TPU v7x, 256 devices: a whole 4x4x8 slice. The times are simulated.
256 devices in a mesh: spec: 16 (over z_lo, x, core), photo: 16 (over y, z_hi).
Axes of the slice: x: 4, y: 4, z: 8 (z_hi: 4, z_lo: 2; z = z_hi * 2 + z_lo), core: 2. Of those that a mesh axis runs over, the one named last changes fastest.
Arguments:
- spec_feat: bfloat16 [131072, 64], P(('spec', 'photo')), may hold values from -2.5 to 2.5
- photo_feat: bfloat16 [16, 16384, 64], P('spec', 'photo'), may hold values from -2.5 to 2.5
- spec_mass: bfloat16 [131072], P(('spec', 'photo')), may hold values from 0.25 to 4
- photo_mass: bfloat16 [16, 16384], P('spec', 'photo'), may hold values from 0.25 to 4
- tile_index: int32 [16, 16, 96], P('spec', 'photo'), may hold values from 0 to 2047, as said below
- tile_count: int32 [16, 16], P('spec', 'photo'), may hold values from 4 to 96, as said below
Outputs:
- grad_spec: float32 [131072, 64], P(('spec', 'photo'))
- grad_photo: float32 [16, 16384, 64], P('spec', 'photo')
Inputs may be any that keep to these rules, and one draw needn't show every extreme that they name: `tile_index`: the first tile_count[s, p] entries of each list are distinct; over all lists, every tile row of every spectroscopic block and every tile column of every photometric block lies in some live tile. Entries past the count are ignored. `tile_count`: some pair of blocks has exactly 96 live tiles.
All inputs are finite; a program needn't handle non-finite values.
Results may differ from a plain program's by a relative error of at most 0.002.
Values may be sent and summed in bfloat16 or wider, within the bound.
No kernel may reach another device: no remote copies, remote signals or barrier semaphores. Data moves between devices by JAX's collectives and lax.ppermute only.
A program may use at most 64 MiB of HBM per device.

v0:
```python
import jax
import jax.numpy as jnp
from jax import lax
from jax.sharding import PartitionSpec as P

TILE = 256
SWEEPS = 2
TEMPER = 16.0
GROUP = 8


def per_device(spec_feat, photo_feat, spec_mass, photo_mass, tile_index, tile_count):
    spec_rows, spec_weights = (
        lax.all_gather(spec_feat, "photo", axis=0, tiled=True),
        lax.all_gather(spec_mass, "photo", axis=0, tiled=True),
    )
    photo_rows, photo_weights = (
        lax.all_gather(photo_feat, "spec", axis=0, tiled=True),
        lax.all_gather(photo_mass, "spec", axis=0, tiled=True),
    )
    feat_width = spec_rows.shape[1]
    spec_count = spec_rows.shape[0]
    photo_count = photo_rows.shape[0] * photo_rows.shape[1]
    tile_rows = spec_count // TILE
    tile_cols = photo_count // TILE
    share_len = photo_feat.shape[1]
    spec_blocks = spec_rows.reshape(tile_rows, TILE, feat_width)
    photo_blocks = photo_rows.reshape(tile_cols, TILE, feat_width)
    spec_squares = jnp.sum(jnp.square(spec_blocks.astype(jnp.float32)), axis=2)
    photo_squares = jnp.sum(jnp.square(photo_blocks.astype(jnp.float32)), axis=2)
    slots = tile_index.reshape(-1)
    count = tile_count.reshape(())
    turns = (count + GROUP - 1) // GROUP

    def tile_group(group):
        first = group * GROUP
        picked = lax.dynamic_slice_in_dim(slots, first, GROUP)
        live = first + jnp.arange(GROUP, dtype=jnp.int32) < count
        rows = picked // tile_cols
        columns = picked % tile_cols
        spec_tiles = spec_blocks[rows]
        photo_tiles = photo_blocks[columns]
        cross = jnp.einsum(
            "gif,gjf->gij", spec_tiles, photo_tiles, preferred_element_type=jnp.float32
        )
        dist = spec_squares[rows][:, :, None] + photo_squares[columns][:, None, :] - 2.0 * cross
        kernel = jnp.where(live[:, None, None], jnp.exp(-dist / TEMPER), jnp.float32(0.0))
        return (rows, columns, spec_tiles, photo_tiles, kernel)

    column_scale = jnp.ones((tile_cols, TILE), jnp.float32)
    row_scale = jnp.ones((tile_rows, TILE), jnp.float32)
    marginal_share = jnp.zeros((share_len,), jnp.float32)
    for sweep in range(SWEEPS):

        def row_step(group, total):
            rows, columns, spec_tiles, photo_tiles, kernel = tile_group(group)
            sums = jnp.sum(kernel * column_scale[columns][:, None, :], axis=2)
            return total.at[rows].add(sums)

        row_part = lax.fori_loop(0, turns, row_step, jnp.zeros((tile_rows, TILE), jnp.float32))
        row_total = lax.psum(row_part, "photo")
        row_scale = spec_weights.astype(jnp.float32).reshape(tile_rows, TILE) / row_total

        def column_step(group, total):
            rows, columns, spec_tiles, photo_tiles, kernel = tile_group(group)
            sums = jnp.sum(row_scale[rows][:, :, None] * kernel, axis=1)
            return total.at[columns].add(sums)

        column_part = lax.fori_loop(
            0, turns, column_step, jnp.zeros((tile_cols, TILE), jnp.float32)
        )
        column_total = lax.psum(column_part, "spec")
        column_scale = photo_weights.astype(jnp.float32).reshape(tile_cols, TILE) / column_total
        marginal = (column_scale * column_total).reshape(-1)
        marginal_share = lax.dynamic_slice_in_dim(
            marginal, lax.axis_index("spec") * share_len, share_len
        )

    def plan_tiles(rows, columns, kernel):
        plan = row_scale[rows][:, :, None] * kernel * column_scale[columns][:, None, :]
        return (plan, plan.astype(jnp.bfloat16))

    def grad_step(group, carry):
        row_sum, spec_acc, photo_acc = carry
        rows, columns, spec_tiles, photo_tiles, kernel = tile_group(group)
        plan, plan_low = plan_tiles(rows, columns, kernel)
        row_sum = row_sum.at[rows].add(jnp.sum(plan, axis=2))
        toward = jnp.einsum(
            "gij,gjf->gif", plan_low, photo_tiles, preferred_element_type=jnp.float32
        ).reshape(GROUP, -1)
        spec_acc = spec_acc.at[rows].add(toward)
        back = jnp.einsum(
            "gij,gif->gjf", plan_low, spec_tiles, preferred_element_type=jnp.float32
        ).reshape(GROUP, -1)
        photo_acc = photo_acc.at[columns].add(back)
        return (row_sum, spec_acc, photo_acc)

    start = (
        jnp.zeros((tile_rows, TILE), jnp.float32),
        jnp.zeros((tile_rows, TILE * feat_width), jnp.float32),
        jnp.zeros((tile_cols, TILE * feat_width), jnp.float32),
    )
    row_sum, spec_acc, photo_acc = lax.fori_loop(0, turns, grad_step, start)
    pulled = spec_acc.reshape(spec_count, feat_width)
    row_marginal = lax.psum(row_sum, "photo")
    spec_term = -2.0 * pulled
    spec_share = lax.psum_scatter(
        spec_term.astype(jnp.bfloat16), "photo", scatter_dimension=0, tiled=True
    ).astype(jnp.float32)
    own_rows = spec_feat.shape[0]
    marginal_rows = lax.dynamic_slice_in_dim(
        row_marginal.reshape(-1), lax.axis_index("photo") * own_rows, own_rows
    )
    spec_share = spec_share + 2.0 * marginal_rows[:, None] * spec_feat.astype(jnp.float32)
    photo_term = -2.0 * photo_acc.reshape(photo_count, feat_width)
    photo_share = lax.psum_scatter(photo_term, "spec", scatter_dimension=0, tiled=True)
    photo_share = photo_share + 2.0 * marginal_share[:, None] * photo_feat[0].astype(jnp.float32)
    return (spec_share, photo_share[None])


def solution(mesh):
    return jax.shard_map(
        per_device,
        mesh=mesh,
        in_specs=(
            P(("spec", "photo"), None),
            P("spec", "photo", None),
            P(("spec", "photo")),
            P("spec", "photo"),
            P("spec", "photo", None),
            P("spec", "photo"),
        ),
        out_specs=(P(("spec", "photo"), None), P("spec", "photo", None)),
        check_vma=False,
    )
```

profile of v0, /device:TPU:8, one launch (start us, length us, event | category | flops | bytes accessed | tf_op | source)
XLA Modules:
  0.0 1373.2 jit_solution(6918769820920343711)
XLA Ops:
  10.0 41.3 %all-gather = bf16[16,1,512]{2,1,0:T(2,128)(2,1)S(1)} all-gather(bf16[1,1,512]{2,1,0:T(2,128)(2,1)S(1)} %reshape.416), channel_id=1, replica_groups=mesh['spec'=16,'photo'=16] {'photo'}, dimensions={0}, use_global_device_ids=true | all-gather | bytes 17408 | tf_op jit(solution)/shard_map/all_gather | solution.py:15
  51.5 19.6 %all-gather.1 = bf16[16,1,1024]{2,1,0:T(2,128)(2,1)S(1)} all-gather(bf16[1,1,1024]{2,1,0:T(2,128)(2,1)} %bitcast.64), channel_id=1, replica_groups=mesh['spec'=16,'photo'=16] {'spec'}, dimensions={0}, use_global_device_ids=true | all-gather | bytes 34816 | tf_op jit(solution)/shard_map/all_gather | solution.py:19
  74.6 28.7 %all-gather.7.cloned.1.call-done = bf16[16,1024,64]{1,2,0:T(8,128)(2,1)} async-done(((bf16[1,1024,64]{1,2,0:T(8,128)(2,1)}), bf16[16,1024,64]{1,2,0:T(8,128)(2,1)}) %all-gather.7.cloned.1.call-update) | async-done | bytes 2097168 | tf_op jit(solution)/shard_map/all_gather | solution.py:18
  105.5 4.8 copy.110
  110.3 23.4 %while.64 = (s32[]{:T(128)}, f32[32,256]{1,0:T(8,128)S(1)}, s32[]{:T(128)}, s32[96]{0:T(128)S(1)}, s32[]{:T(128)}, /*index=5*/f32[32,256]{1,0:T(8,128)S(1)}, f32...) while((s32[]{:T(128)}, f32[32,256]{1,0:T(8,128)S(1)}, ...), condition=%wide.region_5.6_spmd, body=%wide.region_2.5_spmd.sunk | while | flops 71305472 | bytes 1753751 | solution.py:60
  111.7 2.8 gather_fusion.1
  119.5 2.8 gather_fusion.1
  133.7 130.7 %psum.35 = f32[32,256]{1,0:T(8,128)S(1)} all-reduce(f32[32,256]{1,0:T(8,128)S(1)} %get-tuple-element.683), channel_id=1, replica_groups=mesh['spec'=16,'photo'=16] {'photo'}, use_global_device_ids=true, to_apply=%region_6.7 | all-reduce | flops 8192 | bytes 65536 | tf_op jit(solution)/shard_map/psum | solution.py:61
  264.4 23.2 %while.65 = (s32[]{:T(128)}, f32[64,256]{1,0:T(8,128)S(1)}, s32[]{:T(128)}, s32[96]{0:T(128)S(1)}, f32[32,256]{1,0:T(8,128)S(1)}, /*index=5*/s32[]{:T(128)}, f32...) while((s32[]{:T(128)}, f32[64,256]{1,0:T(8,128)S(1)}, ...), condition=%wide.region_10.11_spmd, body=%wide.region_7.10_spmd.sunk | while | flops 71305448 | bytes 1688175 | solution.py:69
  264.6 2.8 gather_fusion.6
  288.6 192.6 %all-reduce.3.cloned.1.call-done = f32[64,256]{1,0:T(8,128)} async-done(((f32[64,256]{1,0:T(8,128)}), f32[64,256]{1,0:T(8,128)}) %all-reduce.3.cloned.1.call-update) | async-done | bytes 65552 | tf_op jit(solution)/shard_map/psum | solution.py:72
  482.0 23.4 %while.66 = (s32[]{:T(128)}, f32[32,256]{1,0:T(8,128)S(1)}, s32[]{:T(128)}, s32[96]{0:T(128)S(1)}, s32[]{:T(128)}, /*index=5*/f32[32,256]{1,0:T(8,128)S(1)}, f32...) while((s32[]{:T(128)}, f32[32,256]{1,0:T(8,128)S(1)}, ...), condition=%wide.region_15.16_spmd, body=%wide.region_12.15_spmd.sunk | while | flops 71305472 | bytes 1688211 | solution.py:60
  491.3 2.8 gather_fusion.11
  505.4 131.4 %psum.37 = f32[32,256]{1,0:T(8,128)S(1)} all-reduce(f32[32,256]{1,0:T(8,128)S(1)} %get-tuple-element.685), channel_id=1, replica_groups=mesh['spec'=16,'photo'=16] {'photo'}, use_global_device_ids=true, to_apply=%region_16.17 | all-reduce | flops 8192 | bytes 65536 | tf_op jit(solution)/shard_map/psum | solution.py:61
  636.8 23.2 %while.67 = (s32[]{:T(128)}, f32[64,256]{1,0:T(8,128)S(1)}, s32[]{:T(128)}, s32[96]{0:T(128)S(1)}, f32[32,256]{1,0:T(8,128)S(1)}, /*index=5*/s32[]{:T(128)}, f32...) while((s32[]{:T(128)}, f32[64,256]{1,0:T(8,128)S(1)}, ...), condition=%wide.region_20.21_spmd, body=%wide.region_17.20_spmd.sunk | while | flops 71305448 | bytes 1688175 | solution.py:69
  660.7 191.8 %all-reduce.5.cloned.1.call-done = f32[64,256]{1,0:T(8,128)} async-done(((f32[64,256]{1,0:T(8,128)}), f32[64,256]{1,0:T(8,128)}) %all-reduce.5.cloned.1.call-update) | async-done | bytes 65552 | tf_op jit(solution)/shard_map/psum | solution.py:72
  855.8 84.9 %while.68 = (s32[]{:T(128)}, f32[32,256]{1,0:T(8,128)S(1)}, f32[32,16384]{1,0:T(8,128)S(1)}, f32[64,16384]{1,0:T(8,128)}, s32[]{:T(128)}, /*index=5*/s32[96]{0:T...) while((s32[]{:T(128)}, f32[32,256]{1,0:T(8,128)S(1)}, ...), condition=%wide.region_27.28_spmd, body=%wide.region_22.27_spmd.sunk | while | flops 206833920 | bytes 12722983 | solution.py:103
  856.2 3.0 gather_fusion.21
  860.4 3.6 gather_fusion.22
  871.8 5.8 scatter_fusion.6
  884.5 3.0 gather_fusion.21
  888.6 3.6 gather_fusion.22
  900.0 5.8 scatter_fusion.6
  912.7 3.0 gather_fusion.21
  916.9 3.6 gather_fusion.22
  928.3 5.8 scatter_fusion.6
  940.9 3.3 convert_element_type.39
  944.2 4.5 broadcast_multiply_fusion
  948.7 7.4 mul.208
  957.4 295.6 %psum.39 = f32[8192]{0:T(1024)S(1)} all-reduce(f32[8192]{0:T(1024)S(1)} %bitcast.62), channel_id=1, replica_groups=mesh['spec'=16,'photo'=16] {'photo'}, use_global_device_ids=true, to_apply=%region_29.30 | all-reduce | flops 8192 | bytes 65536 | tf_op jit(solution)/shard_map/psum | solution.py:105
  1253.1 32.7 %reduce-scatter.3.cloned.1.call-done = bf16[512,64]{1,0:T(8,128)(2,1)} async-done(((bf16[8192,64]{1,0:T(8,128)(2,1)}), bf16[512,64]{1,0:T(8,128)(2,1)}) %reduce-scatter.3.cloned.1.call-update) | async-done | bytes 65552 | tf_op jit(solution)/shard_map/reduce_scatter | solution.py:107
  1287.5 76.6 %reduce-scatter.5.cloned.1.call-done = f32[1024,64]{1,0:T(8,128)} async-done(((f32[16384,64]{1,0:T(8,128)}), f32[1024,64]{1,0:T(8,128)}) %reduce-scatter.5.cloned.1.call-update) | async-done | bytes 262160 | tf_op jit(solution)/shard_map/reduce_scatter | solution.py:116
  (254 shorter events, 147.3 us)
Async XLA Ops:
  7.2 63.9 %all-gather.5.cloned.1.call-start = ((), (), s32[]{:S(2)}) async-start(), calls=%async_computation.2 | async-start | bytes 1114112 | tf_op jit(solution)/shard_map/all_gather | solution.py:14
  7.9 95.4 %all-gather.7.cloned.1.call-start = ((), (), s32[]{:S(2)}) async-start(), calls=%async_computation.3 | async-start | bytes 2228224 | tf_op jit(solution)/shard_map/all_gather | solution.py:18
  8.6 472.5 %all-reduce.3.cloned.1.call-start = ((), (), s32[]{:S(2)}) async-start(), calls=%async_computation.4 | async-start | bytes 131072 | tf_op jit(solution)/shard_map/psum | solution.py:72
  105.5 4.8 copy-start.4
  287.7 0.6 copy-start.2
  288.3 564.2 %all-reduce.5.cloned.1.call-start = ((), (), s32[]{:S(2)}) async-start(), calls=%async_computation.5 | async-start | bytes 131072 | tf_op jit(solution)/shard_map/psum | solution.py:72
  660.0 0.6 copy-start.3
  660.0 193.3 %copy-start = (bf16[32,256,64]{2,1,0:T(8,128)(2,1)}, bf16[32,256,64]{2,1,0:T(8,128)(2,1)S(1)}, u32[]{:S(2)}) copy-start(bf16[32,256,64]{2,1,0:T(8,128)(2,1)S(1)} %get-tuple-element.1442) | copy-start | bytes 3145732
  660.7 625.0 %reduce-scatter.3.cloned.1.call-start = ((), (), s32[]{:S(2)}) async-start(), calls=%async_computation.6 | async-start | bytes 2228224 | tf_op jit(solution)/shard_map/reduce_scatter | solution.py:107
  865.8 2.2 copy-start.1
  894.0 2.2 copy-start.1
  922.3 2.2 copy-start.1
  944.2 420.0 %reduce-scatter.5.cloned.1.call-start = ((), (), s32[]{:S(2)}) async-start(), calls=%async_computation.7 | async-start | bytes 8912896 | tf_op jit(solution)/shard_map/reduce_scatter | solution.py:116
  956.1 0.9 copy-start.5
  956.1 1.1 copy-start.6
Sparse Core Ops, SparseCore 0:
  10.4 55.9 all-gather.4
  68.2 35.0 all-gather.6
  288.4 192.6 all-reduce.2
  660.8 191.6 all-reduce.4
  944.3 341.3 reduce-scatter.2
  1288.1 76.0 reduce-scatter.4
where the time goes:
time: 1380 us; the launch traced here: 1370 us
  blocking collectives  619 us (45%)
  waiting for transfers between devices  524 us (38%)
  local copies, waits for them, and re-layouts  125 us (9%)
  other arithmetic  58.2 us (4%)
  matrix products  30.5 us (2%)
  between operations  15 us (1%)
    psum x2, waiting for transfers between devices, per_device(): column_total = lax.psum(column_part, 'spec')  384 us
    psum x1, blocking collectives, per_device(): row_marginal = lax.psum(row_sum, 'photo')  296 us
    psum x2, blocking collectives, per_device(): row_total = lax.psum(row_part, 'photo')  262 us
    reduce_scatter x1, waiting for transfers between devices, per_device(): lax.psum_scatter(photo_term, 'spec', scatter_dimension=0, tiled=True)  76.6 us
    gather x15, local copies, waits for them, and re-layouts, tile_group(): photo_tiles = photo_blocks[columns]  44.8 us
    all_gather x1, blocking collectives, per_device(): lax.all_gather(spec_mass, 'photo', axis=0, tiled=True)  41.3 us
    reduce_scatter x1, waiting for transfers between devices, per_device(): lax.psum_scatter(spec_term.astype(jnp.bfloat16), 'photo', scatter_dimensi...  32.7 us
    all_gather x1, waiting for transfers between devices, per_device(): lax.all_gather(photo_feat, 'spec', axis=0, tiled=True)  28.7 us
  transfers between devices with their start and end apart: 6, of which 5 were waited for; matrix products, arithmetic and copies ran while one was open for 1% of the time, Pallas kernels for 0%

commit v1 on v0

--- a/solution.py
+++ b/solution.py
@@ -69,7 +69,7 @@
         column_part = lax.fori_loop(
             0, turns, column_step, jnp.zeros((tile_cols, TILE), jnp.float32)
         )
-        column_total = lax.psum(column_part, "spec")
+        column_total = jnp.sum(lax.all_gather(column_part, "spec"), axis=0)
         column_scale = photo_weights.astype(jnp.float32).reshape(tile_cols, TILE) / column_total
         marginal = (column_scale * column_total).reshape(-1)
         marginal_share = lax.dynamic_slice_in_dim(

time: 1380 us -> 1230 us (0.89)
  waiting for transfers between devices: 524 us -> 315 us
  blocking collectives: 619 us -> 673 us
    psum x2 -> x0, waiting for transfers between devices: 384 us -> none  [per_device(): column_total = lax.psum(column_part, 'spec')]
    all_gather x0 -> x2, waiting for transfers between devices: none -> 155 us  [per_device(): column_total = jnp.sum(lax.all_gather(column_part, 'spec'), axis=0)]
    all_gather x1, blocking collectives: 19.6 us -> 74.6 us  [per_device(): lax.all_gather(photo_mass, 'spec', axis=0, tiled=True)]
    all_gather x1, waiting for transfers between devices: 0.01 us -> 14.9 us  [per_device(): lax.all_gather(spec_feat, 'photo', axis=0, tiled=True)]
  transfers between devices with their start and end apart: 6 -> 6, of which waited for: 5 -> 6; matrix products, arithmetic and copies ran while one was open for 1% -> 2% of each run, Pallas kernels for 0% -> 0%
where the time goes in v1:
time: 1230 us; the launch traced here: 1220 us
  blocking collectives  673 us (55%)
  waiting for transfers between devices  315 us (26%)
  local copies, waits for them, and re-layouts  125 us (10%)
  other arithmetic  59.1 us (5%)
  matrix products  30.5 us (2%)
  between operations  15.1 us (1%)
    psum x1, blocking collectives, per_device(): row_marginal = lax.psum(row_sum, 'photo')  295 us
    psum x2, blocking collectives, per_device(): row_total = lax.psum(row_part, 'photo')  262 us
    all_gather x2, waiting for transfers between devices, per_device(): column_total = jnp.sum(lax.all_gather(column_part, 'spec'), axis=0)  155 us
    reduce_scatter x1, waiting for transfers between devices, per_device(): lax.psum_scatter(photo_term, 'spec', scatter_dimension=0, tiled=True)  76.6 us
    all_gather x1, blocking collectives, per_device(): lax.all_gather(photo_mass, 'spec', axis=0, tiled=True)  74.6 us
    gather x15, local copies, waits for them, and re-layouts, tile_group(): photo_tiles = photo_blocks[columns]  44.8 us
    all_gather x1, blocking collectives, per_device(): lax.all_gather(spec_mass, 'photo', axis=0, tiled=True)  41.3 us
    reduce_scatter x1, waiting for transfers between devices, per_device(): lax.psum_scatter(spec_term.astype(jnp.bfloat16), 'photo', scatter_dimensi...  33.8 us
  transfers between devices with their start and end apart: 6, of which 6 were waited for; matrix products, arithmetic and copies ran while one was open for 2% of the time, Pallas kernels for 0%

profile of v1, /device:TPU:8, one launch (start us, length us, event | category | flops | bytes accessed | tf_op | source)
XLA Modules:
  0.0 1219.2 jit_solution(11327606068624133590)
XLA Ops:
  10.0 41.3 %all-gather.2 = bf16[16,1,512]{2,1,0:T(2,128)(2,1)S(1)} all-gather(bf16[1,1,512]{2,1,0:T(2,128)(2,1)S(1)} %reshape.414), channel_id=1, replica_groups=mesh['spec'=16,'photo'=16] {'photo'}, dimensions={0}, use_global_device_ids=true | all-gather | bytes 17408 | tf_op jit(solution)/shard_map/all_gather | solution.py:15
  51.5 14.9 %all-gather.9.cloned.1.call-done = bf16[8192,64]{0,1:T(8,128)(2,1)} async-done(((bf16[512,64]{0,1:T(8,128)(2,1)}), bf16[8192,64]{0,1:T(8,128)(2,1)}) %all-gather.9.cloned.1.call-update) | async-done | bytes 1048592 | tf_op jit(solution)/shard_map/all_gather | solution.py:14
  69.9 32.9 %all-gather.11.cloned.1.call-done = bf16[16,1024,64]{1,2,0:T(8,128)(2,1)} async-done(((bf16[1,1024,64]{1,2,0:T(8,128)(2,1)}), bf16[16,1024,64]{1,2,0:T(8,128)(2,1)}) %all-gather.11.cloned.1.call-update) | async-done | bytes 2097168 | tf_op jit(solution)/shard_map/all_gather | solution.py:18
  105.0 4.8 copy.110
  109.8 23.4 %while.64 = (s32[]{:T(128)}, f32[32,256]{1,0:T(8,128)S(1)}, s32[]{:T(128)}, s32[96]{0:T(128)S(1)}, s32[]{:T(128)}, /*index=5*/f32[32,256]{1,0:T(8,128)S(1)}, f32...) while((s32[]{:T(128)}, f32[32,256]{1,0:T(8,128)S(1)}, ...), condition=%wide.region_5.6_spmd, body=%wide.region_2.5_spmd.sunk | while | flops 71305472 | bytes 1753751 | solution.py:60
  111.2 2.8 gather_fusion.1
  133.2 130.7 %psum.21 = f32[32,256]{1,0:T(8,128)S(1)} all-reduce(f32[32,256]{1,0:T(8,128)S(1)} %get-tuple-element.683), channel_id=1, replica_groups=mesh['spec'=16,'photo'=16] {'photo'}, use_global_device_ids=true, to_apply=%region_6.7 | all-reduce | flops 8192 | bytes 65536 | tf_op jit(solution)/shard_map/psum | solution.py:61
  264.0 23.2 %while.65 = (s32[]{:T(128)}, f32[64,256]{1,0:T(8,128)S(1)}, s32[]{:T(128)}, s32[96]{0:T(128)S(1)}, f32[32,256]{1,0:T(8,128)S(1)}, /*index=5*/s32[]{:T(128)}, f32...) while((s32[]{:T(128)}, f32[64,256]{1,0:T(8,128)S(1)}, ...), condition=%wide.region_10.11_spmd, body=%wide.region_7.10_spmd.sunk | while | flops 71305448 | bytes 1688175 | solution.py:69
  287.9 74.6 %all-gather.3 = bf16[16,1,1024]{2,1,0:T(2,128)(2,1)S(1)} all-gather(bf16[1,1,1024]{2,1,0:T(2,128)(2,1)S(1)} %bitcast.70), channel_id=1, replica_groups=mesh['spec'=16,'photo'=16] {'spec'}, dimensions={0}, use_global_device_ids=true | all-gather | bytes 34816 | tf_op jit(solution)/shard_map/all_gather | solution.py:19
  362.8 40.2 %all-gather.13.cloned.1.call-done = f32[1024,256]{1,0:T(8,128)} async-done(((f32[64,256]{1,0:T(8,128)}), f32[1024,256]{1,0:T(8,128)}) %all-gather.13.cloned.1.call-update) | async-done | bytes 1048592 | tf_op jit(solution)/shard_map/all_gather | solution.py:72
  404.3 23.4 %while.66 = (s32[]{:T(128)}, f32[32,256]{1,0:T(8,128)S(1)}, s32[]{:T(128)}, s32[96]{0:T(128)S(1)}, s32[]{:T(128)}, /*index=5*/f32[32,256]{1,0:T(8,128)S(1)}, f32...) while((s32[]{:T(128)}, f32[32,256]{1,0:T(8,128)S(1)}, ...), condition=%wide.region_15.16_spmd, body=%wide.region_12.15_spmd.sunk | while | flops 71305472 | bytes 1688211 | solution.py:60
  405.8 2.8 gather_fusion.11
  427.7 130.9 %psum.22 = f32[32,256]{1,0:T(8,128)S(1)} all-reduce(f32[32,256]{1,0:T(8,128)S(1)} %get-tuple-element.685), channel_id=1, replica_groups=mesh['spec'=16,'photo'=16] {'photo'}, use_global_device_ids=true, to_apply=%region_16.17 | all-reduce | flops 8192 | bytes 65536 | tf_op jit(solution)/shard_map/psum | solution.py:61
  558.6 23.2 %while.67 = (s32[]{:T(128)}, f32[64,256]{1,0:T(8,128)S(1)}, s32[]{:T(128)}, s32[96]{0:T(128)S(1)}, f32[32,256]{1,0:T(8,128)S(1)}, /*index=5*/s32[]{:T(128)}, f32...) while((s32[]{:T(128)}, f32[64,256]{1,0:T(8,128)S(1)}, ...), condition=%wide.region_20.21_spmd, body=%wide.region_17.20_spmd.sunk | while | flops 71305448 | bytes 1688175 | solution.py:69
  574.3 2.8 gather_fusion.16
  582.6 114.9 %all-gather.15.cloned.1.call-done = f32[1024,256]{1,0:T(8,128)} async-done(((f32[64,256]{1,0:T(8,128)}), f32[1024,256]{1,0:T(8,128)}) %all-gather.15.cloned.1.call-update) | async-done | bytes 1048592 | tf_op jit(solution)/shard_map/all_gather | solution.py:72
  701.3 84.9 %while.68 = (s32[]{:T(128)}, f32[32,256]{1,0:T(8,128)S(1)}, f32[32,16384]{1,0:T(8,128)S(1)}, f32[64,16384]{1,0:T(8,128)}, s32[]{:T(128)}, /*index=5*/s32[96]{0:T...) while((s32[]{:T(128)}, f32[32,256]{1,0:T(8,128)S(1)}, ...), condition=%wide.region_27.28_spmd, body=%wide.region_22.27_spmd.sunk | while | flops 206833920 | bytes 12722983 | solution.py:103
  701.7 3.0 gather_fusion.21
  705.9 3.6 gather_fusion.22
  717.2 5.8 scatter_fusion.6
  730.0 3.0 gather_fusion.21
  734.1 3.6 gather_fusion.22
  745.5 5.8 scatter_fusion.6
  758.2 3.0 gather_fusion.21
  762.4 3.6 gather_fusion.22
  773.8 5.8 scatter_fusion.6
  786.4 3.3 convert_element_type.42
  789.7 4.5 broadcast_multiply_fusion
  794.2 7.4 mul.209
  802.9 295.1 %psum.23 = f32[8192]{0:T(1024)S(1)} all-reduce(f32[8192]{0:T(1024)S(1)} %bitcast.67), channel_id=1, replica_groups=mesh['spec'=16,'photo'=16] {'photo'}, use_global_device_ids=true, to_apply=%region_29.30 | all-reduce | flops 8192 | bytes 65536 | tf_op jit(solution)/shard_map/psum | solution.py:105
  1098.0 33.8 %reduce-scatter.3.cloned.1.call-done = bf16[512,64]{1,0:T(8,128)(2,1)} async-done(((bf16[8192,64]{1,0:T(8,128)(2,1)}), bf16[512,64]{1,0:T(8,128)(2,1)}) %reduce-scatter.3.cloned.1.call-update) | async-done | bytes 65552 | tf_op jit(solution)/shard_map/reduce_scatter | solution.py:107
  1133.6 76.6 %reduce-scatter.5.cloned.1.call-done = f32[1024,64]{1,0:T(8,128)} async-done(((f32[16384,64]{1,0:T(8,128)}), f32[1024,64]{1,0:T(8,128)}) %reduce-scatter.5.cloned.1.call-update) | async-done | bytes 262160 | tf_op jit(solution)/shard_map/reduce_scatter | solution.py:116
  (263 shorter events, 151.1 us)
Async XLA Ops:
  7.2 59.2 %all-gather.9.cloned.1.call-start = ((), (), s32[]{:S(2)}) async-start(), calls=%async_computation.2 | async-start | bytes 1114112 | tf_op jit(solution)/shard_map/all_gather | solution.py:14
  7.9 95.0 %all-gather.11.cloned.1.call-start = ((), (), s32[]{:S(2)}) async-start(), calls=%async_computation.3 | async-start | bytes 2228224 | tf_op jit(solution)/shard_map/all_gather | solution.py:18
  8.6 394.4 %all-gather.13.cloned.1.call-start = ((), (), s32[]{:S(2)}) async-start(), calls=%async_computation.6 | async-start | bytes 1114112 | tf_op jit(solution)/shard_map/all_gather | solution.py:72
  105.0 4.8 copy-start.4
  264.0 23.9 %copy-start.9 = (bf16[1,1024]{1,0:T(2,128)(2,1)S(1)}, bf16[1,1024]{1,0:T(2,128)(2,1)}, u32[]{:S(2)}) copy-start(bf16[1,1024]{1,0:T(2,128)(2,1)} %param.19) | copy-start | bytes 6148
  287.2 0.6 copy-start.2
  287.9 409.6 %all-gather.15.cloned.1.call-start = ((), (), s32[]{:S(2)}) async-start(), calls=%async_computation.7 | async-start | bytes 1114112 | tf_op jit(solution)/shard_map/all_gather | solution.py:72
  362.6 40.4 %copy-start.5 = (bf16[16,1,1024]{2,1,0:T(2,128)(2,1)}, bf16[16,1,1024]{2,1,0:T(2,128)(2,1)S(1)}, u32[]{:S(2)}) copy-start(bf16[16,1,1024]{2,1,0:T(2,128)(2,1)S(1)} %all-gather.3) | copy-start | bytes 98308
  581.9 0.6 copy-start.3
  581.9 117.0 %copy-start = (bf16[32,256,64]{2,1,0:T(8,128)(2,1)}, bf16[32,256,64]{2,1,0:T(8,128)(2,1)S(1)}, u32[]{:S(2)}) copy-start(bf16[32,256,64]{2,1,0:T(8,128)(2,1)S(1)} %get-tuple-element.1440) | copy-start | bytes 3145732
  582.5 549.3 %reduce-scatter.3.cloned.1.call-start = ((), (), s32[]{:S(2)}) async-start(), calls=%async_computation.4 | async-start | bytes 2228224 | tf_op jit(solution)/shard_map/reduce_scatter | solution.py:107
  711.3 2.2 copy-start.1
  739.5 2.2 copy-start.1
  767.8 2.2 copy-start.1
  789.7 420.6 %reduce-scatter.5.cloned.1.call-start = ((), (), s32[]{:S(2)}) async-start(), calls=%async_computation.5 | async-start | bytes 8912896 | tf_op jit(solution)/shard_map/reduce_scatter | solution.py:116
  801.6 0.8 copy-start.6
  801.6 0.9 copy-start.7
  801.6 1.1 copy-start.8
Sparse Core Ops, SparseCore 0:
  10.4 55.9 all-gather.8
  68.2 34.5 all-gather.10
  288.0 114.9 all-gather.12
  582.7 114.8 all-gather.14
  789.8 341.9 reduce-scatter.2
  1134.2 76.0 reduce-scatter.4
